TPU v7x, 32 devices: a whole 2x2x4 slice. The times are simulated.
32 devices in a mesh: clips: 2 (over x), tile: 4 (over y, core), tm: 4 (over z).
Axes of the slice: x: 2, y: 2, z: 4, core: 2. Of those that a mesh axis runs over, the one named last changes fastest.
Arguments:
- clip_frames: bfloat16 [16, 16, 128, 256], P(('clips', 'tm'), 'tile'), parts along dimension 0, may hold values from -6 to 6
- weight_first: bfloat16 [3, 3, 3, 256, 256], replicated, may hold values from -0.078125 to 0.078125
- bias_first: float32 [256], replicated, may hold values from -3 to 3
- weight_second: bfloat16 [3, 3, 3, 256, 256], replicated, may hold values from -0.078125 to 0.078125
- bias_second: float32 [256], replicated, may hold values from -3 to 3
Outputs:
- pooled_frames: bfloat16 [8, 16, 128, 256], P(('clips', 'tm'), 'tile'), parts along dimension 0
There are 2 independent parts, one for each index of `clips`. A program takes and returns all parts, laid end to end along the dimension named above; an argument that names none is the same for every part. Nothing has to cross between parts.
All inputs are finite; a program needn't handle non-finite values.
Results may differ from a plain program's by a relative error of at most 0.0029.
Values may be sent and summed in bfloat16 or wider, within the bound.
No kernel may reach another device: no remote copies, remote signals or barrier semaphores. Data moves between devices by JAX's collectives and lax.ppermute only.
A program may use at most 128 MiB of HBM per device.

v0:
```python
import functools

import jax
import jax.numpy as jnp
from jax import lax
from jax.experimental import pallas as pl
from jax.experimental.pallas import tpu as pltpu
from jax.sharding import PartitionSpec as P


VMEM = pl.BlockSpec(memory_space=pltpu.VMEM)
HBM = pl.BlockSpec(memory_space=pltpu.HBM)


def call(body, outs, args, flops, in_specs=None, out_specs=None, scratch=(), aliases=None):
    return pl.pallas_call(
        body,
        out_shape=outs,
        in_specs=in_specs or [VMEM] * len(args),
        out_specs=out_specs or [VMEM] * len(outs),
        scratch_shapes=scratch,
        input_output_aliases=aliases or {},
        compiler_params=pltpu.CompilerParams(vmem_limit_bytes=16 << 20),
        cost_estimate=pl.CostEstimate(flops=flops, bytes_accessed=0, transcendentals=0),
    )(*args)


def flat(value):
    return value.reshape(-1, value.shape[-1])


def row_taps(slab, rows):
    return [flat(slab[p : p + rows]) for p in range(3)]


def shifted_columns(part, q):
    if q == 1:
        return part
    cols = part.shape[1]
    col = lax.broadcasted_iota(jnp.int32, part.shape, 1)
    edge, steps = (0, 1) if q == 0 else (cols - 1, cols - 1)
    return jnp.where(col == edge, 0.0, pltpu.roll(part, steps, 1))


def convolved(lhs, weights, rows, cols):
    stacked = jnp.concatenate(lhs, axis=1)
    total = None
    for q in range(3):
        taps = jnp.concatenate([w[q] for w in weights], axis=0)
        part = jnp.dot(stacked, taps, preferred_element_type=jnp.float32)
        part = shifted_columns(part.reshape(rows, cols, part.shape[-1]), q)
        total = part if total is None else total + part
    return total


def convolved_pair(first, second, shared, extra, rows, cols):
    lhs = jnp.concatenate([jnp.concatenate(taps, axis=1) for taps in (first, second)], axis=0)
    count = rows * cols
    total = None
    for q in range(3):
        taps = [jnp.concatenate([w[q] for w in weights], axis=0) for weights in (shared, extra)]
        part = jnp.dot(lhs, taps[0], preferred_element_type=jnp.float32)
        more = jnp.dot(lhs[count:], taps[1], preferred_element_type=jnp.float32)
        part = jnp.concatenate([part[:count] + more, part[count:]], axis=0)
        part = shifted_columns(part.reshape(2 * rows, cols, part.shape[-1]), q)
        total = part if total is None else total + part
    return total[:rows], total[rows:]


def parity():
    return lax.rem(lax.axis_index("tile"), 2)


def either(first, second):
    even = parity() == 0
    return jnp.concatenate([jnp.where(even, a, b) for a, b in zip(first, second)], axis=0)


def own_edge(own, side):
    odd = parity()
    last = own.shape[0] - 2
    return own[pl.ds((odd if side == 0 else 1 - odd) * last, 2)]


def outer_slab(outer, own, tiles):
    tile = lax.axis_index("tile")
    beyond = (tile == 0) | ((tile == tiles - 1) & (parity() == 1))
    outer = jnp.where(beyond, jnp.zeros_like(outer), outer)
    edge = own_edge(own, 0)
    return either([outer, edge], [edge, outer])


def inner_slab(inner, own):
    edge = own_edge(own, 1)
    return either([edge, inner], [inner, edge])


def places(rows):
    odd = parity()
    return pl.ds(2, rows - 2), pl.ds((1 - odd) * rows, 2), pl.ds(odd * rows, 2)


def weight_rows(w_ref, a):
    return [[w_ref[a, p, q] for q in range(3)] for p in range(3)]


def silu_rows(value, start, rows, tiles):
    hidden = (0.5 * value * (1.0 + jnp.tanh(0.5 * value))).astype(jnp.bfloat16)
    row = lax.broadcasted_iota(jnp.int32, hidden.shape, 0) + start
    row = row + lax.axis_index("tile") * rows - 1
    inside = (row >= 0) & (row < tiles * rows)
    return jnp.where(inside, hidden, jnp.zeros_like(hidden))


def edges_body(x_ref, own_ref, outer_ref, inner_ref, sem):
    copy = pltpu.make_async_copy(x_ref, own_ref, sem)
    copy.start()
    copy.wait()
    for f in range(2):
        outer_ref[f] = own_edge(own_ref.at[f], 0)
        inner_ref[f] = own_edge(own_ref.at[f], 1)


def turn_body(m_ref, inner_ref):
    for f in range(2):
        inner_ref[f] = own_edge(m_ref.at[f], 1)


def own_sums(slabs, w_ref, b_ref, acc0_ref, acc1_ref):
    rows, cols = acc0_ref.shape[:2]
    taps = [row_taps(slab, rows) for slab in slabs]
    shared, extra = weight_rows(w_ref, 2), weight_rows(w_ref, 1)
    late, early = convolved_pair(taps[1], taps[0], shared, extra, rows, cols)
    acc0_ref[...] = b_ref[...] + early
    acc1_ref[...] = b_ref[...] + late


def own_near_body(x_ref, inner_ref, w_ref, b_ref, acc0_ref, acc1_ref):
    even = parity() == 0
    slabs = []
    for f in range(2):
        below = jnp.concatenate([x_ref[f], inner_ref[f]], axis=0)
        above = jnp.concatenate([inner_ref[f], x_ref[f]], axis=0)
        slabs.append(jnp.where(even, below, above))
    own_sums(slabs, w_ref, b_ref, acc0_ref, acc1_ref)


def own_far_body(tiles, x_ref, outer_ref, w_ref, b_ref, acc0_ref, acc1_ref):
    slabs = [outer_slab(outer_ref[f], x_ref.at[f], tiles) for f in range(2)]
    own_sums(slabs, w_ref, b_ref, acc0_ref, acc1_ref)


def hidden(slab, bases, place, w_ref, tiles, whole, h0_ref, h1_ref):
    rows, cols = h0_ref.shape[:2]
    started = lax.axis_index("tm") > 0

    def store(sums):
        for h_ref, total in zip((h0_ref, h1_ref), sums):
            h_ref[...] = silu_rows(total, place.start, whole, tiles)

    @pl.when(started)
    def _():
        taps = [row_taps(slab(f), rows) for f in range(2)]
        shared, extra = weight_rows(w_ref, 0), weight_rows(w_ref, 1)
        products = convolved_pair(taps[0], taps[1], shared, extra, rows, cols)
        store([base() + product for base, product in zip(bases, products)])

    @pl.when(jnp.logical_not(started))
    def _():
        store([base() for base in bases])


def from_near(acc_ref, start, rows):
    return lambda: acc_ref[pl.ds(start, rows)]


def middle_body(tiles, m_ref, w_ref, _, acc0_ref, acc1_ref, h0_ref, h1_ref):
    rows = m_ref.shape[1]
    start = 2 * parity()
    bases = [from_near(acc_ref, start, rows - 2) for acc_ref in (acc0_ref, acc1_ref)]
    place = places(rows)[0]
    hidden(lambda f: m_ref[f], bases, place, w_ref, tiles, rows, h0_ref, h1_ref)


def partial_rows(times, h0, h1, v_ref, rows, cols, send_ref):
    has_next = lax.axis_index("tm") < times - 1

    @pl.when(has_next)
    def _():
        both = (h0.astype(jnp.float32) + h1.astype(jnp.float32)).astype(jnp.bfloat16)
        taps = row_taps(both, rows) + row_taps(h1, rows)
        part = convolved(taps, weight_rows(v_ref, 0) + weight_rows(v_ref, 1), rows, cols)
        send_ref[...] = part.astype(jnp.bfloat16)

    @pl.when(jnp.logical_not(has_next))
    def _():
        send_ref[...] = jnp.zeros_like(send_ref)


def near_body(
    tiles, times, m_ref, inner_ref, w_ref, v_ref, acc0_ref, acc1_ref, mid0_ref, mid1_ref,
    send_ref, h0_ref, h1_ref,
):
    rows, cols = m_ref.shape[1:3]
    start = (1 - parity()) * (rows - 2)
    bases = [from_near(acc_ref, start, 2) for acc_ref in (acc0_ref, acc1_ref)]
    place = places(rows)[1]

    def slab(f):
        return inner_slab(inner_ref[f], m_ref.at[f])

    def beside(h_ref, mid_ref):
        below = jnp.concatenate([mid_ref[...], h_ref[...]], axis=0)
        above = jnp.concatenate([h_ref[...], mid_ref[...]], axis=0)
        return jnp.where(parity() == 0, below, above)

    hidden(slab, bases, place, w_ref, tiles, rows, h0_ref, h1_ref)
    h0, h1 = beside(h0_ref, mid0_ref), beside(h1_ref, mid1_ref)
    partial_rows(times, h0, h1, v_ref, rows - 2, cols, send_ref)


def far_body(
    tiles, times, m_ref, outer_ref, w_ref, v_ref, acc0_ref, acc1_ref, mid0_ref, mid1_ref,
    send_ref, h0_ref, h1_ref,
):
    rows, cols = m_ref.shape[1:3]
    odd = parity()

    def slab(f):
        return outer_slab(outer_ref[f], m_ref.at[f], tiles)

    def beside(h_ref, mid_ref):
        middle = mid_ref[pl.ds(odd * (rows - 4), 2)]
        return either([h_ref[...], middle], [middle, h_ref[...]])

    bases = [lambda: acc0_ref[...], lambda: acc1_ref[...]]
    hidden(slab, bases, places(rows)[2], w_ref, tiles, rows, h0_ref, h1_ref)
    h0, h1 = beside(h0_ref, mid0_ref), beside(h1_ref, mid1_ref)
    partial_rows(times, h0, h1, v_ref, 2, cols, send_ref)


def rest_body(
    x_ref, mid0_ref, mid1_ref, near0_ref, near1_ref, far0_ref, far1_ref, v_ref, b_ref, out_ref,
    h0_ref, h1_ref,
):
    rows, cols = x_ref.shape[1:3]
    middle, near, far = places(rows)
    h0_ref[middle], h1_ref[middle] = mid0_ref[...], mid1_ref[...]
    h0_ref[near], h1_ref[near] = near0_ref[...], near1_ref[...]
    h0_ref[far], h1_ref[far] = far0_ref[...], far1_ref[...]
    h0, h1 = row_taps(h0_ref[...], rows), row_taps(h1_ref[...], rows)
    weights = weight_rows(v_ref, 1) + 2 * weight_rows(v_ref, 2)
    part = convolved(h0 + h0 + h1, weights, rows, cols)
    total = x_ref[0].astype(jnp.float32) + x_ref[1].astype(jnp.float32) + part
    out_ref[0] = total * 0.5 + b_ref[...]


def join(rest_ref, part_ref, out_ref, start, made_ref, sem):
    part = part_ref[...].astype(jnp.float32)
    part = jnp.where(lax.axis_index("tm") == 0, jnp.zeros_like(part), part)
    place = pl.ds(start, part.shape[0])
    made_ref[...] = (rest_ref[0, place] + 0.5 * part).astype(jnp.bfloat16)
    copy = pltpu.make_async_copy(made_ref, out_ref.at[0, place], sem)
    copy.start()
    copy.wait()


def join_near_body(rest_ref, part_ref, out_ref, made_ref, sem):
    join(rest_ref, part_ref, out_ref, 2 * (1 - parity()), made_ref, sem)


def join_far_body(rest_ref, part_ref, _, out_ref, made_ref, sem):
    join(rest_ref, part_ref, out_ref, parity() * (rest_ref.shape[1] - 2), made_ref, sem)


def block(x, weight_first, bias_first, weight_second, bias_second):
    _, rows, cols, channels = x.shape
    clips, tiles, times = (lax.axis_size(axis) for axis in ("clips", "tile", "tm"))
    forward = [(i, i + 1) for i in range(times - 1)]
    ring = forward + [(times - 1, 0)]
    inner_pairs = [(i, i + 1) for i in range(0, tiles - 1, 2)]
    outer_pairs = [(i, i + 1) for i in range(1, tiles - 1, 2)]
    inner_pairs += [(j, i) for i, j in inner_pairs]
    outer_pairs += [(j, i) for i, j in outer_pairs]
    paired = {i for i, _ in outer_pairs}
    unpaired = [i for i in range(tiles) if i not in paired]
    outer_full = [(c * tiles + i, c * tiles + j) for c in range(clips) for i, j in outer_pairs]
    outer_full += [(c * tiles + i, (c + 1) % clips * tiles + i) for c in range(clips) for i in unpaired]
    diagonal = [(i * times + s, j * times + t) for i, j in outer_pairs for s, t in forward]

    def frames(*lead, dtype=jnp.bfloat16):
        return jax.ShapeDtypeStruct((*lead, cols, channels), dtype)

    f32 = jnp.float32
    earlier = lax.ppermute(x, "tm", ring)
    x, outer_edge, inner_edge = call(
        edges_body,
        [frames(2, rows), frames(2, 2), frames(2, 2)],
        (pltpu.with_memory_space_constraint(x, pltpu.HBM),),
        10**10,
        in_specs=[HBM],
        scratch=[pltpu.SemaphoreType.DMA(())],
    )
    inner = lax.ppermute(inner_edge, "tile", inner_pairs)
    outer = lax.ppermute(outer_edge, ("clips", "tile"), outer_full)
    corner = lax.ppermute(outer_edge, ("tile", "tm"), diagonal)

    bias_first = bias_first.reshape(1, 1, -1)
    bias_second = bias_second.reshape(1, 1, -1)
    unit = 2 * 9 * channels * channels * cols
    wide = rows + 2
    sums0, sums1 = call(
        own_near_body,
        [frames(rows, dtype=f32), frames(rows, dtype=f32)],
        (x, inner, weight_first, bias_first),
        3 * unit * rows,
    )
    far0, far1 = call(
        functools.partial(own_far_body, tiles),
        [frames(2, dtype=f32), frames(2, dtype=f32)],
        (x, outer, weight_first, bias_first),
        0,
    )
    (inner_edge,) = call(turn_body, [frames(2, 2)], (earlier,), 0)
    inner_corner = lax.ppermute(inner_edge, "tile", inner_pairs)

    mid0, mid1 = call(
        functools.partial(middle_body, tiles),
        [frames(rows - 2), frames(rows - 2)],
        (earlier, weight_first, weight_second, sums0, sums1),
        0,
    )
    near_send, near0, near1 = call(
        functools.partial(near_body, tiles, times),
        [frames(rows - 2), frames(2), frames(2)],
        (earlier, inner_corner, weight_first, weight_second, sums0, sums1, mid0, mid1),
        0,
    )
    near_part = lax.ppermute(near_send, "tm", ring)
    far_send, last0, last1 = call(
        functools.partial(far_body, tiles, times),
        [frames(2), frames(2), frames(2)],
        (earlier, corner, weight_first, weight_second, far0, far1, mid0, mid1),
        0,
    )
    far_part = lax.ppermute(far_send, "tm", forward)
    (rest,) = call(
        rest_body,
        [frames(1, rows, dtype=f32)],
        (x, mid0, mid1, near0, near1, last0, last1, weight_second, bias_second),
        3 * unit * rows,
        scratch=[pltpu.VMEM((wide, cols, channels), jnp.bfloat16)] * 2,
    )
    (pooled,) = call(
        join_near_body,
        [frames(1, rows)],
        (rest, near_part),
        0,
        out_specs=[HBM],
        scratch=[pltpu.VMEM((rows - 2, cols, channels), jnp.bfloat16), pltpu.SemaphoreType.DMA(())],
    )
    (pooled,) = call(
        join_far_body,
        [frames(1, rows)],
        (rest, far_part, pooled),
        0,
        in_specs=[VMEM, VMEM, HBM],
        out_specs=[HBM],
        scratch=[pltpu.VMEM((2, cols, channels), jnp.bfloat16), pltpu.SemaphoreType.DMA(())],
        aliases={2: 0},
    )
    return pooled


def solution(mesh):
    in_specs = (P(("clips", "tm"), "tile", None, None), P(), P(), P(), P())
    out_specs = P(("clips", "tm"), "tile", None, None)
    return jax.shard_map(block, mesh=mesh, in_specs=in_specs, out_specs=out_specs, check_vma=False)
```

profile of v0, /device:TPU:0, one launch (start us, length us, event | category | flops | bytes accessed | tf_op | source)
XLA Modules:
  0.0 36.3 jit_solution(17960984705495873531)
XLA Ops:
  0.0 0.0 copy-start
  0.0 0.0 copy-start.2
  0.0 3.1 %collective-permute-start = (bf16[2,4,128,256]{3,2,1,0:T(8,128)(2,1)}, bf16[2,4,128,256]{3,2,1,0:T(8,128)(2,1)S(1)}, u32[]{:S(2)}, u32[]{:S(2)}) collective-permute-start(bf16[2,4,128,256]{3,2,1,0:T(8,128)(2,1)} %x_ref.1), channel_id=1, source_target_pairs={{0,1},{1,2},{2,3},{3,0},{4,5},{5,6},{6,7},{7,4},{8,9},{9,10},{10,1... | collective-permute-start | bytes 1572872 | tf_op jit(solution)/shard_map/ppermute | solution.py:295
  3.1 1.1 %shard_map.55 = (bf16[2,4,128,256]{3,2,1,0:T(8,128)(2,1)S(1)}, bf16[2,2,128,256]{3,2,1,0:T(8,128)(2,1)S(1)}, bf16[2,2,128,256]{3,2,1,0:T(8,128)(2,1)S(1)}) custom-call(bf16[2,4,128,256]{3,2,1,0:T(8,128)(2,1)} %x_ref.1), custom_call_target="tpu_custom_call" | custom-call | flops 10000000000 | tf_op jit(solution)/shard_map/pallas_call | solution.py:16
  4.2 1.6 %collective-permute-start.4 = (bf16[2,2,128,256]{3,2,1,0:T(8,128)(2,1)S(1)}, bf16[2,2,128,256]{3,2,1,0:T(8,128)(2,1)S(1)}, u32[]{:S(2)}, u32[]{:S(2)}) collective-permute-start(bf16[2,2,128,256]{3,2,1,0:T(8,128)(2,1)S(1)} %get-tuple-element.28), channel_id=1, source_target_pairs={{4,8},{8,4},{20,24},{24,20},{0,16},{12,28},{16,0},{28,12},{5,9},{9... | collective-permute-start | bytes 786440 | tf_op jit(solution)/shard_map/ppermute | solution.py:305
  5.7 0.1 collective-permute-start.1
  5.9 0.7 %collective-permute-start.3 = (bf16[2,2,128,256]{3,2,1,0:T(8,128)(2,1)S(1)}, bf16[2,2,128,256]{3,2,1,0:T(8,128)(2,1)S(1)}, u32[]{:S(2)}, u32[]{:S(2)}) collective-permute-start(bf16[2,2,128,256]{3,2,1,0:T(8,128)(2,1)S(1)} %get-tuple-element.28), channel_id=1, source_target_pairs={{4,9},{5,10},{6,11},{8,5},{9,6},{10,7},{20,25},{21,26},{22,27},{24... | collective-permute-start | bytes 786440 | tf_op jit(solution)/shard_map/ppermute | solution.py:306
  6.6 10.7 %collective-permute-done.m_ref = bf16[2,4,128,256]{3,2,1,0:T(8,128)(2,1)S(1)} collective-permute-done((bf16[2,4,128,256]{3,2,1,0:T(8,128)(2,1)}, bf16[2,4,128,256]{3,2,1,0:T(8,128)(2,1)S(1)}, u32[]{:S(2)}, u32[]{:S(2)}) %collective-permute-start) | collective-permute-done | bytes 524320 | tf_op jit(solution)/shard_map/ppermute | solution.py:295
  17.2 0.1 collective-permute-start.2
  17.3 0.0 collective-permute-done.4.outer_ref
  17.3 0.0 copy-done
  17.3 0.0 copy-done.2
  17.3 1.1 %shard_map.60 = (f32[2,128,256]{2,1,0:T(8,128)S(1)}, f32[2,128,256]{2,1,0:T(8,128)S(1)}) custom-call(bf16[2,4,128,256]{3,2,1,0:T(8,128)(2,1)S(1)} %get-tuple-element.20.x_ref, bf16[2,2,128,256]{3,2,1,0:T(8,128)(2,1)S(1)} %collective-permute-done.4.outer_ref, bf16[3,3,3,256,256]{4,3,2,1,0:T(8,128)(2,1)S(1)} %copy-done, f32[1,1,256]{2,1,0:T(1,128)S(1)} %bitcast.2), custom_call_target="tpu_custom_call" | custom-call | tf_op jit(solution)/shard_map/pallas_call | solution.py:16
  18.4 0.0 copy-start.1
  18.5 0.0 collective-permute-done.1.inner_ref
  18.5 2.0 %shard_map.56 = (f32[4,128,256]{2,1,0:T(8,128)S(1)}, f32[4,128,256]{2,1,0:T(8,128)S(1)}) custom-call(bf16[2,4,128,256]{3,2,1,0:T(8,128)(2,1)S(1)} %get-tuple-element.20.x_ref, bf16[2,2,128,256]{3,2,1,0:T(8,128)(2,1)S(1)} %collective-permute-done.1.inner_ref, bf16[3,3,3,256,256]{4,3,2,1,0:T(8,128)(2,1)S(1)} %copy-done, f32[1,1,256]{2,1,0:T(1,128)S(1)} %bitcast.3), custom_call_target="tpu_custom_call" | custom-call | flops 1811939328 | tf_op jit(solution)/shard_map/pallas_call | solution.py:16
  20.5 0.0 copy-done.1
  20.5 0.1 shard_map.57
  20.6 0.0 collective-permute-done.3.outer_ref
  20.6 0.9 %shard_map.61 = (bf16[2,128,256]{2,1,0:T(8,128)(2,1)S(1)}, bf16[2,128,256]{2,1,0:T(8,128)(2,1)S(1)}, bf16[2,128,256]{2,1,0:T(8,128)(2,1)S(1)}) custom-call(bf16[2,4,128,256]{3,2,1,0:T(8,128)(2,1)S(1)} %collective-permute-done.m_ref, bf16[2,2,128,256]{3,2,1,0:T(8,128)(2,1)S(1)} %collective-permute-done.3.outer_ref, bf16[3,3,3,256,256]{4,3,2,1,0:T(8,128)(2,1)S(1)} %copy-done, ...), custom_call_target="tpu_custom_call" | custom-call | tf_op jit(solution)/shard_map/pallas_call | solution.py:16
  21.6 0.0 copy-start.3
  21.6 4.8 %collective-permute-start.5 = (bf16[2,128,256]{2,1,0:T(8,128)(2,1)S(1)}, bf16[2,128,256]{2,1,0:T(8,128)(2,1)S(1)}, u32[]{:S(2)}, u32[]{:S(2)}) collective-permute-start(bf16[2,128,256]{2,1,0:T(8,128)(2,1)S(1)} %get-tuple-element.33), channel_id=1, source_target_pairs={{0,1},{1,2},{2,3},{4,5},{5,6},{6,7},{8,9},{9,10},{10,11},{12,13},{... | collective-permute-start | bytes 393224 | tf_op jit(solution)/shard_map/ppermute | solution.py:346
  26.4 0.0 collective-permute-done.2.inner_ref
  26.4 0.9 %shard_map.59 = (bf16[2,128,256]{2,1,0:T(8,128)(2,1)S(1)}, bf16[2,128,256]{2,1,0:T(8,128)(2,1)S(1)}, bf16[2,128,256]{2,1,0:T(8,128)(2,1)S(1)}) custom-call(bf16[2,4,128,256]{3,2,1,0:T(8,128)(2,1)S(1)} %collective-permute-done.m_ref, bf16[2,2,128,256]{3,2,1,0:T(8,128)(2,1)S(1)} %collective-permute-done.2.inner_ref, bf16[3,3,3,256,256]{4,3,2,1,0:T(8,128)(2,1)S(1)} %copy-done, ...), custom_call_target="tpu_custom_call" | custom-call | tf_op jit(solution)/shard_map/pallas_call | solution.py:16
  27.4 2.6 %collective-permute-start.6 = (bf16[2,128,256]{2,1,0:T(8,128)(2,1)S(1)}, bf16[2,128,256]{2,1,0:T(8,128)(2,1)S(1)}, u32[]{:S(2)}, u32[]{:S(2)}) collective-permute-start(bf16[2,128,256]{2,1,0:T(8,128)(2,1)S(1)} %get-tuple-element.34), channel_id=1, source_target_pairs={{0,1},{1,2},{2,3},{3,0},{4,5},{5,6},{6,7},{7,4},{8,9},{9,10},{10,1... | collective-permute-start | bytes 393224 | tf_op jit(solution)/shard_map/ppermute | solution.py:339
  30.0 0.0 copy-done.3
  30.0 2.0 %shard_map.62.rest_ref = f32[1,4,128,256]{3,2,1,0:T(8,128)S(1)} custom-call(bf16[2,4,128,256]{3,2,1,0:T(8,128)(2,1)S(1)} %get-tuple-element.20.x_ref, bf16[2,128,256]{2,1,0:T(8,128)(2,1)S(1)} %get-tuple-element.24.mid0_ref, bf16[2,128,256]{2,1,0:T(8,128)(2,1)S(1)} %get-tuple-element.25.mid1_ref, bf16[2,128,256]{2,1,0:T(8,128)(2,1)S(1)} %get-tuple-element.26.near0_ref, ...), custom_call_target="tpu_custom_call" | custom-call | flops 1811939328 | tf_op jit(solution)/shard_map/pallas_call | solution.py:16
  32.1 2.8 %collective-permute-done.6.part_ref = bf16[2,128,256]{2,1,0:T(8,128)(2,1)S(1)} collective-permute-done((bf16[2,128,256]{2,1,0:T(8,128)(2,1)S(1)}, bf16[2,128,256]{2,1,0:T(8,128)(2,1)S(1)}, u32[]{:S(2)}, u32[]{:S(2)}) %collective-permute-start.6) | collective-permute-done | bytes 131104 | tf_op jit(solution)/shard_map/ppermute | solution.py:339
  34.8 0.7 %shard_map.63._ = bf16[1,4,128,256]{3,2,1,0:T(8,128)(2,1)} custom-call(f32[1,4,128,256]{3,2,1,0:T(8,128)S(1)} %shard_map.62.rest_ref, bf16[2,128,256]{2,1,0:T(8,128)(2,1)S(1)} %collective-permute-done.6.part_ref), custom_call_target="tpu_custom_call" | custom-call | tf_op jit(solution)/shard_map/pallas_call | solution.py:16
  35.6 0.0 collective-permute-done.5.part_ref
  35.6 0.7 %shard_map.64 = bf16[1,4,128,256]{3,2,1,0:T(8,128)(2,1)} custom-call(f32[1,4,128,256]{3,2,1,0:T(8,128)S(1)} %shard_map.62.rest_ref, bf16[2,128,256]{2,1,0:T(8,128)(2,1)S(1)} %collective-permute-done.5.part_ref, bf16[1,4,128,256]{3,2,1,0:T(8,128)(2,1)} %shard_map.63._), custom_call_target="tpu_custom_call", output_to_operand_aliasing={{}: (2, {})} | custom-call | tf_op jit(solution)/shard_map/pallas_call | solution.py:16
  (1 shorter events, 0.0 us)
Async XLA Ops:
  0.0 17.3 %copy-start = (bf16[3,3,3,256,256]{4,3,2,1,0:T(8,128)(2,1)S(1)}, bf16[3,3,3,256,256]{4,3,2,1,0:T(8,128)(2,1)}, u32[]{:S(2)}) copy-start(bf16[3,3,3,256,256]{4,3,2,1,0:T(8,128)(2,1)} %w_ref.9) | copy-start | bytes 10616836
  0.0 17.3 %copy-start.2 = (f32[256]{0:T(256)S(1)}, f32[256]{0:T(256)}, u32[]{:S(2)}) copy-start(f32[256]{0:T(256)} %param.7) | copy-start | bytes 3076
  0.0 17.2 %collective-permute-start = (bf16[2,4,128,256]{3,2,1,0:T(8,128)(2,1)}, bf16[2,4,128,256]{3,2,1,0:T(8,128)(2,1)S(1)}, u32[]{:S(2)}, u32[]{:S(2)}) collective-permute-start(bf16[2,4,128,256]{3,2,1,0:T(8,128)(2,1)} %x_ref.1), channel_id=1, source_target_pairs={{0,1},{1,2},{2,3},{3,0},{4,5},{5,6},{6,7},{7,4},{8,9},{9,10},{10,1... | collective-permute-start | bytes 1572872 | tf_op jit(solution)/shard_map/ppermute | solution.py:295
  4.2 13.1 %collective-permute-start.4 = (bf16[2,2,128,256]{3,2,1,0:T(8,128)(2,1)S(1)}, bf16[2,2,128,256]{3,2,1,0:T(8,128)(2,1)S(1)}, u32[]{:S(2)}, u32[]{:S(2)}) collective-permute-start(bf16[2,2,128,256]{3,2,1,0:T(8,128)(2,1)S(1)} %get-tuple-element.28), channel_id=1, source_target_pairs={{4,8},{8,4},{20,24},{24,20},{0,16},{12,28},{16,0},{28,12},{5,9},{9... | collective-permute-start | bytes 786440 | tf_op jit(solution)/shard_map/ppermute | solution.py:305
  5.7 12.7 %collective-permute-start.1 = (bf16[2,2,128,256]{3,2,1,0:T(8,128)(2,1)S(1)}, bf16[2,2,128,256]{3,2,1,0:T(8,128)(2,1)S(1)}, u32[]{:S(2)}, u32[]{:S(2)}) collective-permute-start(bf16[2,2,128,256]{3,2,1,0:T(8,128)(2,1)S(1)} %get-tuple-element.21), channel_id=1, source_target_pairs={{0,4},{8,12},{4,0},{12,8},{1,5},{9,13},{5,1},{13,9},{2,6},{10,14},... | collective-permute-start | bytes 786440 | tf_op jit(solution)/shard_map/ppermute | solution.py:304
  5.9 14.7 %collective-permute-start.3 = (bf16[2,2,128,256]{3,2,1,0:T(8,128)(2,1)S(1)}, bf16[2,2,128,256]{3,2,1,0:T(8,128)(2,1)S(1)}, u32[]{:S(2)}, u32[]{:S(2)}) collective-permute-start(bf16[2,2,128,256]{3,2,1,0:T(8,128)(2,1)S(1)} %get-tuple-element.28), channel_id=1, source_target_pairs={{4,9},{5,10},{6,11},{8,5},{9,6},{10,7},{20,25},{21,26},{22,27},{24... | collective-permute-start | bytes 786440 | tf_op jit(solution)/shard_map/ppermute | solution.py:306
  17.2 9.2 %collective-permute-start.2 = (bf16[2,2,128,256]{3,2,1,0:T(8,128)(2,1)S(1)}, bf16[2,2,128,256]{3,2,1,0:T(8,128)(2,1)S(1)}, u32[]{:S(2)}, u32[]{:S(2)}) collective-permute-start(bf16[2,2,128,256]{3,2,1,0:T(8,128)(2,1)S(1)} %shard_map.58), channel_id=1, source_target_pairs={{0,4},{8,12},{4,0},{12,8},{1,5},{9,13},{5,1},{13,9},{2,6},{10,14},... | collective-permute-start | bytes 786440 | tf_op jit(solution)/shard_map/ppermute | solution.py:325
  18.4 2.0 %copy-start.1 = (bf16[3,3,3,256,256]{4,3,2,1,0:T(8,128)(2,1)S(1)}, bf16[3,3,3,256,256]{4,3,2,1,0:T(8,128)(2,1)}, u32[]{:S(2)}) copy-start(bf16[3,3,3,256,256]{4,3,2,1,0:T(8,128)(2,1)} %v_ref.5) | copy-start | bytes 10616836
  21.6 8.4 %copy-start.3 = (f32[256]{0:T(256)S(1)}, f32[256]{0:T(256)}, u32[]{:S(2)}) copy-start(f32[256]{0:T(256)} %param.9) | copy-start | bytes 3076
  21.6 14.0 %collective-permute-start.5 = (bf16[2,128,256]{2,1,0:T(8,128)(2,1)S(1)}, bf16[2,128,256]{2,1,0:T(8,128)(2,1)S(1)}, u32[]{:S(2)}, u32[]{:S(2)}) collective-permute-start(bf16[2,128,256]{2,1,0:T(8,128)(2,1)S(1)} %get-tuple-element.33), channel_id=1, source_target_pairs={{0,1},{1,2},{2,3},{4,5},{5,6},{6,7},{8,9},{9,10},{10,11},{12,13},{... | collective-permute-start | bytes 393224 | tf_op jit(solution)/shard_map/ppermute | solution.py:346
  27.4 7.4 %collective-permute-start.6 = (bf16[2,128,256]{2,1,0:T(8,128)(2,1)S(1)}, bf16[2,128,256]{2,1,0:T(8,128)(2,1)S(1)}, u32[]{:S(2)}, u32[]{:S(2)}) collective-permute-start(bf16[2,128,256]{2,1,0:T(8,128)(2,1)S(1)} %get-tuple-element.34), channel_id=1, source_target_pairs={{0,1},{1,2},{2,3},{3,0},{4,5},{5,6},{6,7},{7,4},{8,9},{9,10},{10,1... | collective-permute-start | bytes 393224 | tf_op jit(solution)/shard_map/ppermute | solution.py:339
where the time goes:
time: 36.5 us; the launch traced here: 36.3 us
  waiting for transfers between devices  13.4 us (37%)
  starting transfers between devices  12.9 us (35%)
  Pallas kernels  9.7 us (27%)
    ppermute x1, waiting for transfers between devices, block(): earlier = lax.ppermute(x, 'tm', ring)  10.7 us
    pallas_call x10, Pallas kernels, call(): pl.pallas_call(body, out_shape=outs, in_specs=in_specs or [VMEM] * len(ar...  9.7 us
    ppermute x1, starting transfers between devices, block(): far_part = lax.ppermute(far_send, 'tm', forward)  4.82 us
    ppermute x1, starting transfers between devices, block(): earlier = lax.ppermute(x, 'tm', ring)  3.05 us
    ppermute x1, waiting for transfers between devices, block(): near_part = lax.ppermute(near_send, 'tm', ring)  2.77 us
    ppermute x1, starting transfers between devices, block(): near_part = lax.ppermute(near_send, 'tm', ring)  2.64 us
    ppermute x1, starting transfers between devices, block(): outer = lax.ppermute(outer_edge, ('clips', 'tile'), outer_full)  1.56 us
  transfers between devices with their start and end apart: 7, of which 2 were waited for; matrix products, arithmetic and copies ran while one was open for 0% of the time, Pallas kernels for 25%

commit v1 on v0

--- a/solution.py
+++ b/solution.py
@@ -105,18 +105,22 @@
 
 
 def silu_rows(value, start, rows, tiles):
-    hidden = (0.5 * value * (1.0 + jnp.tanh(0.5 * value))).astype(jnp.bfloat16)
+    half = 0.5 * value
+    hidden = (half + half * jnp.tanh(half)).astype(jnp.bfloat16)
     row = lax.broadcasted_iota(jnp.int32, hidden.shape, 0) + start
     row = row + lax.axis_index("tile") * rows - 1
     inside = (row >= 0) & (row < tiles * rows)
     return jnp.where(inside, hidden, jnp.zeros_like(hidden))
 
 
-def edges_body(x_ref, own_ref, outer_ref, inner_ref, sem):
-    copy = pltpu.make_async_copy(x_ref, own_ref, sem)
-    copy.start()
-    copy.wait()
-    for f in range(2):
+def edges_body(x_ref, own_ref, outer_ref, inner_ref, sems):
+    copies = [
+        pltpu.make_async_copy(x_ref.at[f], own_ref.at[f], sems.at[f]) for f in range(2)
+    ]
+    for copy in copies:
+        copy.start()
+    for f, copy in enumerate(copies):
+        copy.wait()
         outer_ref[f] = own_edge(own_ref.at[f], 0)
         inner_ref[f] = own_edge(own_ref.at[f], 1)
 
@@ -299,7 +303,7 @@
         (pltpu.with_memory_space_constraint(x, pltpu.HBM),),
         10**10,
         in_specs=[HBM],
-        scratch=[pltpu.SemaphoreType.DMA(())],
+        scratch=[pltpu.SemaphoreType.DMA((2,))],
     )
     inner = lax.ppermute(inner_edge, "tile", inner_pairs)
     outer = lax.ppermute(outer_edge, ("clips", "tile"), outer_full)

time: 36.5 us -> 36.5 us (level)
  no operation moved by 1% of the time
where the time goes in v1:
time: 36.5 us; the launch traced here: 36.3 us
  waiting for transfers between devices  13.5 us (37%)
  starting transfers between devices  13 us (36%)
  Pallas kernels  9.65 us (26%)
    ppermute x1, waiting for transfers between devices, block(): earlier = lax.ppermute(x, 'tm', ring)  10.7 us
    pallas_call x10, Pallas kernels, call(): pl.pallas_call(body, out_shape=outs, in_specs=in_specs or [VMEM] * len(ar...  9.65 us
    ppermute x1, starting transfers between devices, block(): far_part = lax.ppermute(far_send, 'tm', forward)  4.83 us
    ppermute x1, starting transfers between devices, block(): earlier = lax.ppermute(x, 'tm', ring)  3.05 us
    ppermute x1, waiting for transfers between devices, block(): near_part = lax.ppermute(near_send, 'tm', ring)  2.78 us
    ppermute x1, starting transfers between devices, block(): near_part = lax.ppermute(near_send, 'tm', ring)  2.64 us
    ppermute x1, starting transfers between devices, block(): outer = lax.ppermute(outer_edge, ('clips', 'tile'), outer_full)  1.56 us
  transfers between devices with their start and end apart: 7, of which 2 were waited for; matrix products, arithmetic and copies ran while one was open for 0% of the time, Pallas kernels for 25%

profile of v1, /device:TPU:0, one launch (start us, length us, event | category | flops | bytes accessed | tf_op | source)
XLA Modules:
  0.0 36.3 jit_solution(15160276680430232140)
XLA Ops:
  0.0 0.0 copy-start
  0.0 0.0 copy-start.2
  0.0 3.1 %collective-permute-start = (bf16[2,4,128,256]{3,2,1,0:T(8,128)(2,1)}, bf16[2,4,128,256]{3,2,1,0:T(8,128)(2,1)S(1)}, u32[]{:S(2)}, u32[]{:S(2)}) collective-permute-start(bf16[2,4,128,256]{3,2,1,0:T(8,128)(2,1)} %x_ref.1), channel_id=1, source_target_pairs={{0,1},{1,2},{2,3},{3,0},{4,5},{5,6},{6,7},{7,4},{8,9},{9,10},{10,1... | collective-permute-start | bytes 1572872 | tf_op jit(solution)/shard_map/ppermute | solution.py:299
  3.1 1.1 %shard_map.55 = (bf16[2,4,128,256]{3,2,1,0:T(8,128)(2,1)S(1)}, bf16[2,2,128,256]{3,2,1,0:T(8,128)(2,1)S(1)}, bf16[2,2,128,256]{3,2,1,0:T(8,128)(2,1)S(1)}) custom-call(bf16[2,4,128,256]{3,2,1,0:T(8,128)(2,1)} %x_ref.1), custom_call_target="tpu_custom_call" | custom-call | flops 10000000000 | tf_op jit(solution)/shard_map/pallas_call | solution.py:16
  4.1 1.6 %collective-permute-start.4 = (bf16[2,2,128,256]{3,2,1,0:T(8,128)(2,1)S(1)}, bf16[2,2,128,256]{3,2,1,0:T(8,128)(2,1)S(1)}, u32[]{:S(2)}, u32[]{:S(2)}) collective-permute-start(bf16[2,2,128,256]{3,2,1,0:T(8,128)(2,1)S(1)} %get-tuple-element.28), channel_id=1, source_target_pairs={{4,8},{8,4},{20,24},{24,20},{0,16},{12,28},{16,0},{28,12},{5,9},{9... | collective-permute-start | bytes 786440 | tf_op jit(solution)/shard_map/ppermute | solution.py:309
  5.7 0.1 collective-permute-start.1
  5.8 0.7 %collective-permute-start.3 = (bf16[2,2,128,256]{3,2,1,0:T(8,128)(2,1)S(1)}, bf16[2,2,128,256]{3,2,1,0:T(8,128)(2,1)S(1)}, u32[]{:S(2)}, u32[]{:S(2)}) collective-permute-start(bf16[2,2,128,256]{3,2,1,0:T(8,128)(2,1)S(1)} %get-tuple-element.28), channel_id=1, source_target_pairs={{4,9},{5,10},{6,11},{8,5},{9,6},{10,7},{20,25},{21,26},{22,27},{24... | collective-permute-start | bytes 786440 | tf_op jit(solution)/shard_map/ppermute | solution.py:310
  6.5 10.7 %collective-permute-done.m_ref = bf16[2,4,128,256]{3,2,1,0:T(8,128)(2,1)S(1)} collective-permute-done((bf16[2,4,128,256]{3,2,1,0:T(8,128)(2,1)}, bf16[2,4,128,256]{3,2,1,0:T(8,128)(2,1)S(1)}, u32[]{:S(2)}, u32[]{:S(2)}) %collective-permute-start) | collective-permute-done | bytes 524320 | tf_op jit(solution)/shard_map/ppermute | solution.py:299
  17.2 0.1 collective-permute-start.2
  17.3 0.0 collective-permute-done.4.outer_ref
  17.3 0.0 copy-done
  17.3 0.0 copy-done.2
  17.3 1.1 %shard_map.60 = (f32[2,128,256]{2,1,0:T(8,128)S(1)}, f32[2,128,256]{2,1,0:T(8,128)S(1)}) custom-call(bf16[2,4,128,256]{3,2,1,0:T(8,128)(2,1)S(1)} %get-tuple-element.20.x_ref, bf16[2,2,128,256]{3,2,1,0:T(8,128)(2,1)S(1)} %collective-permute-done.4.outer_ref, bf16[3,3,3,256,256]{4,3,2,1,0:T(8,128)(2,1)S(1)} %copy-done, f32[1,1,256]{2,1,0:T(1,128)S(1)} %bitcast.2), custom_call_target="tpu_custom_call" | custom-call | tf_op jit(solution)/shard_map/pallas_call | solution.py:16
  18.4 0.0 copy-start.1
  18.5 0.0 collective-permute-done.1.inner_ref
  18.5 2.0 %shard_map.56 = (f32[4,128,256]{2,1,0:T(8,128)S(1)}, f32[4,128,256]{2,1,0:T(8,128)S(1)}) custom-call(bf16[2,4,128,256]{3,2,1,0:T(8,128)(2,1)S(1)} %get-tuple-element.20.x_ref, bf16[2,2,128,256]{3,2,1,0:T(8,128)(2,1)S(1)} %collective-permute-done.1.inner_ref, bf16[3,3,3,256,256]{4,3,2,1,0:T(8,128)(2,1)S(1)} %copy-done, f32[1,1,256]{2,1,0:T(1,128)S(1)} %bitcast.3), custom_call_target="tpu_custom_call" | custom-call | flops 1811939328 | tf_op jit(solution)/shard_map/pallas_call | solution.py:16
  20.5 0.0 copy-done.1
  20.5 0.1 shard_map.57
  20.6 0.0 collective-permute-done.3.outer_ref
  20.6 0.9 %shard_map.61 = (bf16[2,128,256]{2,1,0:T(8,128)(2,1)S(1)}, bf16[2,128,256]{2,1,0:T(8,128)(2,1)S(1)}, bf16[2,128,256]{2,1,0:T(8,128)(2,1)S(1)}) custom-call(bf16[2,4,128,256]{3,2,1,0:T(8,128)(2,1)S(1)} %collective-permute-done.m_ref, bf16[2,2,128,256]{3,2,1,0:T(8,128)(2,1)S(1)} %collective-permute-done.3.outer_ref, bf16[3,3,3,256,256]{4,3,2,1,0:T(8,128)(2,1)S(1)} %copy-done, ...), custom_call_target="tpu_custom_call" | custom-call | tf_op jit(solution)/shard_map/pallas_call | solution.py:16
  21.6 0.0 copy-start.3
  21.6 4.8 %collective-permute-start.5 = (bf16[2,128,256]{2,1,0:T(8,128)(2,1)S(1)}, bf16[2,128,256]{2,1,0:T(8,128)(2,1)S(1)}, u32[]{:S(2)}, u32[]{:S(2)}) collective-permute-start(bf16[2,128,256]{2,1,0:T(8,128)(2,1)S(1)} %get-tuple-element.33), channel_id=1, source_target_pairs={{0,1},{1,2},{2,3},{4,5},{5,6},{6,7},{8,9},{9,10},{10,11},{12,13},{... | collective-permute-start | bytes 393224 | tf_op jit(solution)/shard_map/ppermute | solution.py:350
  26.4 0.0 collective-permute-done.2.inner_ref
  26.5 0.9 %shard_map.59 = (bf16[2,128,256]{2,1,0:T(8,128)(2,1)S(1)}, bf16[2,128,256]{2,1,0:T(8,128)(2,1)S(1)}, bf16[2,128,256]{2,1,0:T(8,128)(2,1)S(1)}) custom-call(bf16[2,4,128,256]{3,2,1,0:T(8,128)(2,1)S(1)} %collective-permute-done.m_ref, bf16[2,2,128,256]{3,2,1,0:T(8,128)(2,1)S(1)} %collective-permute-done.2.inner_ref, bf16[3,3,3,256,256]{4,3,2,1,0:T(8,128)(2,1)S(1)} %copy-done, ...), custom_call_target="tpu_custom_call" | custom-call | tf_op jit(solution)/shard_map/pallas_call | solution.py:16
  27.4 2.6 %collective-permute-start.6 = (bf16[2,128,256]{2,1,0:T(8,128)(2,1)S(1)}, bf16[2,128,256]{2,1,0:T(8,128)(2,1)S(1)}, u32[]{:S(2)}, u32[]{:S(2)}) collective-permute-start(bf16[2,128,256]{2,1,0:T(8,128)(2,1)S(1)} %get-tuple-element.34), channel_id=1, source_target_pairs={{0,1},{1,2},{2,3},{3,0},{4,5},{5,6},{6,7},{7,4},{8,9},{9,10},{10,1... | collective-permute-start | bytes 393224 | tf_op jit(solution)/shard_map/ppermute | solution.py:343
  30.1 0.0 copy-done.3
  30.1 2.0 %shard_map.62.rest_ref = f32[1,4,128,256]{3,2,1,0:T(8,128)S(1)} custom-call(bf16[2,4,128,256]{3,2,1,0:T(8,128)(2,1)S(1)} %get-tuple-element.20.x_ref, bf16[2,128,256]{2,1,0:T(8,128)(2,1)S(1)} %get-tuple-element.24.mid0_ref, bf16[2,128,256]{2,1,0:T(8,128)(2,1)S(1)} %get-tuple-element.25.mid1_ref, bf16[2,128,256]{2,1,0:T(8,128)(2,1)S(1)} %get-tuple-element.26.near0_ref, ...), custom_call_target="tpu_custom_call" | custom-call | flops 1811939328 | tf_op jit(solution)/shard_map/pallas_call | solution.py:16
  32.1 2.8 %collective-permute-done.6.part_ref = bf16[2,128,256]{2,1,0:T(8,128)(2,1)S(1)} collective-permute-done((bf16[2,128,256]{2,1,0:T(8,128)(2,1)S(1)}, bf16[2,128,256]{2,1,0:T(8,128)(2,1)S(1)}, u32[]{:S(2)}, u32[]{:S(2)}) %collective-permute-start.6) | collective-permute-done | bytes 131104 | tf_op jit(solution)/shard_map/ppermute | solution.py:343
  34.9 0.7 %shard_map.63._ = bf16[1,4,128,256]{3,2,1,0:T(8,128)(2,1)} custom-call(f32[1,4,128,256]{3,2,1,0:T(8,128)S(1)} %shard_map.62.rest_ref, bf16[2,128,256]{2,1,0:T(8,128)(2,1)S(1)} %collective-permute-done.6.part_ref), custom_call_target="tpu_custom_call" | custom-call | tf_op jit(solution)/shard_map/pallas_call | solution.py:16
  35.6 0.0 collective-permute-done.5.part_ref
  35.6 0.7 %shard_map.64 = bf16[1,4,128,256]{3,2,1,0:T(8,128)(2,1)} custom-call(f32[1,4,128,256]{3,2,1,0:T(8,128)S(1)} %shard_map.62.rest_ref, bf16[2,128,256]{2,1,0:T(8,128)(2,1)S(1)} %collective-permute-done.5.part_ref, bf16[1,4,128,256]{3,2,1,0:T(8,128)(2,1)} %shard_map.63._), custom_call_target="tpu_custom_call", output_to_operand_aliasing={{}: (2, {})} | custom-call | tf_op jit(solution)/shard_map/pallas_call | solution.py:16
  (1 shorter events, 0.0 us)
Async XLA Ops:
  0.0 17.3 %copy-start = (bf16[3,3,3,256,256]{4,3,2,1,0:T(8,128)(2,1)S(1)}, bf16[3,3,3,256,256]{4,3,2,1,0:T(8,128)(2,1)}, u32[]{:S(2)}) copy-start(bf16[3,3,3,256,256]{4,3,2,1,0:T(8,128)(2,1)} %w_ref.9) | copy-start | bytes 10616836
  0.0 17.3 %copy-start.2 = (f32[256]{0:T(256)S(1)}, f32[256]{0:T(256)}, u32[]{:S(2)}) copy-start(f32[256]{0:T(256)} %param.7) | copy-start | bytes 3076
  0.0 17.2 %collective-permute-start = (bf16[2,4,128,256]{3,2,1,0:T(8,128)(2,1)}, bf16[2,4,128,256]{3,2,1,0:T(8,128)(2,1)S(1)}, u32[]{:S(2)}, u32[]{:S(2)}) collective-permute-start(bf16[2,4,128,256]{3,2,1,0:T(8,128)(2,1)} %x_ref.1), channel_id=1, source_target_pairs={{0,1},{1,2},{2,3},{3,0},{4,5},{5,6},{6,7},{7,4},{8,9},{9,10},{10,1... | collective-permute-start | bytes 1572872 | tf_op jit(solution)/shard_map/ppermute | solution.py:299
  4.1 13.2 %collective-permute-start.4 = (bf16[2,2,128,256]{3,2,1,0:T(8,128)(2,1)S(1)}, bf16[2,2,128,256]{3,2,1,0:T(8,128)(2,1)S(1)}, u32[]{:S(2)}, u32[]{:S(2)}) collective-permute-start(bf16[2,2,128,256]{3,2,1,0:T(8,128)(2,1)S(1)} %get-tuple-element.28), channel_id=1, source_target_pairs={{4,8},{8,4},{20,24},{24,20},{0,16},{12,28},{16,0},{28,12},{5,9},{9... | collective-permute-start | bytes 786440 | tf_op jit(solution)/shard_map/ppermute | solution.py:309
  5.7 12.8 %collective-permute-start.1 = (bf16[2,2,128,256]{3,2,1,0:T(8,128)(2,1)S(1)}, bf16[2,2,128,256]{3,2,1,0:T(8,128)(2,1)S(1)}, u32[]{:S(2)}, u32[]{:S(2)}) collective-permute-start(bf16[2,2,128,256]{3,2,1,0:T(8,128)(2,1)S(1)} %get-tuple-element.21), channel_id=1, source_target_pairs={{0,4},{8,12},{4,0},{12,8},{1,5},{9,13},{5,1},{13,9},{2,6},{10,14},... | collective-permute-start | bytes 786440 | tf_op jit(solution)/shard_map/ppermute | solution.py:308
  5.8 14.8 %collective-permute-start.3 = (bf16[2,2,128,256]{3,2,1,0:T(8,128)(2,1)S(1)}, bf16[2,2,128,256]{3,2,1,0:T(8,128)(2,1)S(1)}, u32[]{:S(2)}, u32[]{:S(2)}) collective-permute-start(bf16[2,2,128,256]{3,2,1,0:T(8,128)(2,1)S(1)} %get-tuple-element.28), channel_id=1, source_target_pairs={{4,9},{5,10},{6,11},{8,5},{9,6},{10,7},{20,25},{21,26},{22,27},{24... | collective-permute-start | bytes 786440 | tf_op jit(solution)/shard_map/ppermute | solution.py:310
  17.2 9.2 %collective-permute-start.2 = (bf16[2,2,128,256]{3,2,1,0:T(8,128)(2,1)S(1)}, bf16[2,2,128,256]{3,2,1,0:T(8,128)(2,1)S(1)}, u32[]{:S(2)}, u32[]{:S(2)}) collective-permute-start(bf16[2,2,128,256]{3,2,1,0:T(8,128)(2,1)S(1)} %shard_map.58), channel_id=1, source_target_pairs={{0,4},{8,12},{4,0},{12,8},{1,5},{9,13},{5,1},{13,9},{2,6},{10,14},... | collective-permute-start | bytes 786440 | tf_op jit(solution)/shard_map/ppermute | solution.py:329
  18.4 2.0 %copy-start.1 = (bf16[3,3,3,256,256]{4,3,2,1,0:T(8,128)(2,1)S(1)}, bf16[3,3,3,256,256]{4,3,2,1,0:T(8,128)(2,1)}, u32[]{:S(2)}) copy-start(bf16[3,3,3,256,256]{4,3,2,1,0:T(8,128)(2,1)} %v_ref.5) | copy-start | bytes 10616836
  21.6 8.5 %copy-start.3 = (f32[256]{0:T(256)S(1)}, f32[256]{0:T(256)}, u32[]{:S(2)}) copy-start(f32[256]{0:T(256)} %param.9) | copy-start | bytes 3076
  21.6 14.0 %collective-permute-start.5 = (bf16[2,128,256]{2,1,0:T(8,128)(2,1)S(1)}, bf16[2,128,256]{2,1,0:T(8,128)(2,1)S(1)}, u32[]{:S(2)}, u32[]{:S(2)}) collective-permute-start(bf16[2,128,256]{2,1,0:T(8,128)(2,1)S(1)} %get-tuple-element.33), channel_id=1, source_target_pairs={{0,1},{1,2},{2,3},{4,5},{5,6},{6,7},{8,9},{9,10},{10,11},{12,13},{... | collective-permute-start | bytes 393224 | tf_op jit(solution)/shard_map/ppermute | solution.py:350
  27.4 7.5 %collective-permute-start.6 = (bf16[2,128,256]{2,1,0:T(8,128)(2,1)S(1)}, bf16[2,128,256]{2,1,0:T(8,128)(2,1)S(1)}, u32[]{:S(2)}, u32[]{:S(2)}) collective-permute-start(bf16[2,128,256]{2,1,0:T(8,128)(2,1)S(1)} %get-tuple-element.34), channel_id=1, source_target_pairs={{0,1},{1,2},{2,3},{3,0},{4,5},{5,6},{6,7},{7,4},{8,9},{9,10},{10,1... | collective-permute-start | bytes 393224 | tf_op jit(solution)/shard_map/ppermute | solution.py:343
